TPU v7x, 128 devices: a whole 4x4x4 slice. The times are simulated.
128 devices in a mesh: section: 8 (over x, core), seq: 16 (over z, y).
Axes of the slice: x: 4, y: 4, z: 4, core: 2. Of those that a mesh axis runs over, the one named last changes fastest.
Arguments:
- residual: bfloat16 [8, 4096, 2048], P('section', 'seq'), may hold values from -6 to 6
- w_qkv: bfloat16 [8, 2048, 6144], P('section', 'seq'), may hold values from -0.125 to 0.125
- w_beta: bfloat16 [8, 2048, 16], P('section', 'seq'), may hold values from -0.125 to 0.125
- beta_bias: float32 [8, 16], P('section'), may hold values from -8 to 2
- norm_gain: float32 [8, 2048], P('section'), may hold values from 0.1 to 1.9
- out_gain: float32 [8, 128], P('section'), may hold values from 0.1 to 1.9
- state_in: float32 [8, 16, 128, 128], P('section'), may hold values from -6 to 6
- doc_start: int32 [2, 8], P(None, 'section'), may hold values from 0 to 64, as said below
Outputs:
- stream_out: bfloat16 [8, 4096, 2048], P('section', 'seq')
Inputs may be any that keep to these rules, and one draw needn't show every extreme that they name: `doc_start`: 64 means no new document in that micro-batch.
All inputs are finite; a program needn't handle non-finite values.
Results may differ from a plain program's by a relative error of at most 0.03.
Values may be sent and summed in bfloat16 or wider, within the bound.
No kernel may reach another device: no remote copies, remote signals or barrier semaphores. Data moves between devices by JAX's collectives and lax.ppermute only.
A program may use at most 192 MiB of HBM per device.

v0:
```python
import jax
import jax.numpy as jnp
from jax import lax
from jax.sharding import PartitionSpec as P

HEADS = 16
HD = 128
GROUP = 64
TICKS = 2
FULL_PRECISION = lax.Precision.HIGHEST


def from_behind(value, axis, by):
    count = lax.axis_size(axis)
    pairs = [(i, i + by) for i in range(count) if 0 <= i + by < count]
    return lax.ppermute(value, axis, pairs)


def from_root(value, axis, source):
    kept = jnp.where(lax.axis_index(axis) == source, value, 0).astype(value.dtype)
    return lax.psum(kept, axis)


def passed_along(value, axis, by):
    count = lax.axis_size(axis)
    return lax.ppermute(value, axis, [(i, (i + by) % count) for i in range(count)])


def unit_norm(projected):
    return projected * lax.rsqrt(jnp.sum(projected * projected, axis=-1, keepdims=True) + 1e-06)


def block_solve(key_rows, values, beta_rows):
    block_len = key_rows.shape[-2]
    intersections = jnp.einsum("ghik,ghjk->ghij", key_rows, key_rows, precision=FULL_PRECISION)
    system = jnp.tril(intersections * beta_rows[..., :, None], -1) + jnp.eye(
        block_len, dtype=jnp.float32
    )
    right_side = jnp.concatenate(
        [values * beta_rows[..., None], key_rows * beta_rows[..., None]], axis=-1
    )
    solved = lax.linalg.triangular_solve(
        system, right_side, left_side=True, lower=True, unit_diagonal=True
    )
    head_width = values.shape[-1]
    return (solved[..., :head_width], solved[..., head_width:])


def prepare(stream, weight_qkv, weight_beta, head_bias, in_gain):
    row_count = stream.shape[0]
    widened = stream.astype(jnp.float32)
    normed = (
        widened * lax.rsqrt(jnp.mean(widened * widened, axis=-1, keepdims=True) + 1e-05) * in_gain
    ).astype(jnp.bfloat16)
    projected = jnp.dot(normed, weight_qkv, preferred_element_type=jnp.float32).reshape(
        row_count, 3, HEADS, HD
    )
    queries = unit_norm(projected[:, 0]).astype(jnp.bfloat16)
    key_rows = unit_norm(projected[:, 1]).astype(jnp.bfloat16)
    values = projected[:, 2].astype(jnp.bfloat16)
    beta_rows = jax.nn.sigmoid(
        jnp.dot(normed, weight_beta, preferred_element_type=jnp.float32) + head_bias
    )
    blocks = row_count // GROUP

    def to_blocks(tensor):
        return tensor.astype(jnp.float32).reshape(blocks, GROUP, HEADS, HD).transpose(0, 2, 1, 3)

    beta_blk = beta_rows.reshape(blocks, GROUP, HEADS).transpose(0, 2, 1)
    key_block = to_blocks(key_rows)
    inject, weights = block_solve(key_block, to_blocks(values), beta_blk)
    return (to_blocks(queries), key_block, inject, weights, widened)


def run_blocks(queries, key_rows, inject, weights, current_state, doc_block, first_block):
    block_count = queries.shape[0]
    block_len = queries.shape[2]
    causal = jnp.tril(jnp.ones((block_len, block_len), jnp.float32))

    def run_advance(current_state, pieces):
        query_block, key_block, inject_block, weight_block, block_index = pieces
        current_state = jnp.where(
            block_index == doc_block, jnp.zeros_like(current_state), current_state
        )
        delta_values = inject_block - jnp.einsum(
            "jxy,jyu->jxu", weight_block, current_state, precision=FULL_PRECISION
        )
        attention_scores = (
            jnp.einsum("hik,hjk->hij", query_block, key_block, precision=FULL_PRECISION) * causal
        )
        block_result = jnp.einsum(
            "jxy,jyu->jxu", query_block, current_state, precision=FULL_PRECISION
        ) + jnp.einsum("ucd,udo->uco", attention_scores, delta_values, precision=FULL_PRECISION)
        current_state = current_state + jnp.einsum(
            "plq,plw->pqw", key_block, delta_values, precision=FULL_PRECISION
        )
        return (current_state, block_result)

    block_ids = first_block + jnp.arange(block_count, dtype=jnp.int32)
    return lax.scan(run_advance, current_state, (queries, key_rows, inject, weights, block_ids))


def transitions(key_rows, inject, weights, doc_block, first_block):
    head_count = key_rows.shape[1]
    head_width = key_rows.shape[3]
    block_count = key_rows.shape[0]
    identity = jnp.broadcast_to(
        jnp.eye(head_width, dtype=jnp.float32), (head_count, head_width, head_width)
    )

    def transitions_advance(maps, pieces):
        decay_matrix, start_offset = maps
        key_block, inject_block, weight_block, block_index = pieces
        keep_flag = block_index != doc_block
        decay_matrix = jnp.where(keep_flag, decay_matrix, jnp.zeros_like(decay_matrix))
        start_offset = jnp.where(keep_flag, start_offset, jnp.zeros_like(start_offset))
        decay_matrix = decay_matrix - jnp.einsum(
            "plq,plw->pqw",
            key_block,
            jnp.einsum("jxy,jyu->jxu", weight_block, decay_matrix, precision=FULL_PRECISION),
            precision=FULL_PRECISION,
        )
        start_offset = start_offset + jnp.einsum(
            "plq,plw->pqw",
            key_block,
            inject_block
            - jnp.einsum("jxy,jyu->jxu", weight_block, start_offset, precision=FULL_PRECISION),
            precision=FULL_PRECISION,
        )
        return ((decay_matrix, start_offset), None)

    block_ids = first_block + jnp.arange(block_count, dtype=jnp.int32)
    maps, unused = lax.scan(
        transitions_advance,
        (identity, jnp.zeros_like(identity)),
        (key_rows, inject, weights, block_ids),
    )
    return maps


def apply_map(maps, given_state):
    return jnp.einsum("hij,hjk->hik", maps[0], given_state, precision=FULL_PRECISION) + maps[1]


def compose(earlier, latter):
    return (
        jnp.einsum("hij,hjk->hik", latter[0], earlier[0], precision=FULL_PRECISION),
        jnp.einsum("hij,hjk->hik", latter[0], earlier[1], precision=FULL_PRECISION) + latter[1],
    )


def finish(widened, block_result, head_gain):
    blocks = block_result.shape[0]
    mixed = block_result.transpose(0, 2, 1, 3).reshape(blocks * GROUP, HEADS, HD)
    mixed = mixed * lax.rsqrt(jnp.mean(mixed * mixed, axis=-1, keepdims=True) + 1e-05) * head_gain
    return (widened + mixed.reshape(blocks * GROUP, HEADS * HD)).astype(jnp.bfloat16)


def shards(residual, w_qkv, w_beta, beta_bias, norm_gain, out_gain, state_in, doc_start):
    weight_qkv, weight_beta = (
        lax.all_gather(w_qkv[0], "seq", axis=0, tiled=True),
        lax.all_gather(w_beta[0], "seq", axis=0, tiled=True),
    )
    seq_count = lax.axis_size("seq")
    position = lax.axis_index("seq")
    stream = residual[0]
    given_state = state_in[0]
    blocks = stream.shape[0] // GROUP
    first_block = position * blocks
    outputs = stream
    identity = jnp.broadcast_to(jnp.eye(HD, dtype=jnp.float32), (HEADS, HD, HD))
    empty_map = jnp.stack([identity, jnp.zeros_like(identity)])
    for tick_index in range(TICKS):
        doc_block = doc_start[tick_index, 0]
        queries, key_rows, inject, weights, widened = prepare(
            stream, weight_qkv, weight_beta, beta_bias[0], norm_gain[0]
        )
        maps = transitions(key_rows, inject, weights, doc_block, first_block)

        def hop_once(hop_index, carried_map):
            joined = compose((carried_map[0], carried_map[1]), maps)
            passed = from_behind(
                jnp.stack([joined[0], joined[1]]).astype(jnp.bfloat16), "seq", 1
            ).astype(jnp.float32)
            return jnp.where(position == 0, empty_map, passed)

        prefix_map = lax.fori_loop(0, seq_count - 1, hop_once, empty_map)
        prefix = (prefix_map[0], prefix_map[1])
        entry_state = apply_map(prefix, given_state)
        final_state, block_result = run_blocks(
            queries, key_rows, inject, weights, entry_state, doc_block, first_block
        )
        outputs = finish(widened, block_result, out_gain[0])
        if tick_index + 1 < TICKS:
            given_state = from_root(final_state.astype(jnp.bfloat16), "seq", seq_count - 1).astype(
                final_state.dtype
            )
            stream = passed_along(outputs, "section", 1)
    return outputs[None]


def solution(mesh):
    return jax.shard_map(
        shards,
        mesh=mesh,
        in_specs=(
            P("section", "seq", None),
            P("section", "seq", None),
            P("section", "seq", None),
            P("section", None),
            P("section", None),
            P("section", None),
            P("section", None, None, None),
            P(None, "section"),
        ),
        out_specs=P("section", "seq", None),
        check_vma=False,
    )
```

profile of v0, /device:TPU:34, one launch (start us, length us, event | category | flops | bytes accessed | tf_op | source)
XLA Modules:
  0.0 2081.2 jit_solution(3336317457587673220)
XLA Ops:
  7.3 24.4 %all-gather.1 = bf16[1,2048,16]{1,2,0:T(8,128)(2,1)S(1)} all-gather(bf16[1,128,16]{1,2,0:T(8,128)(2,1)} %param.24), channel_id=3, replica_groups=mesh['section'=8,'seq'=16] {'seq'}, dimensions={1}, use_global_device_ids=true | all-gather | bytes 69632 | tf_op jit(solution)/shard_map/all_gather | solution.py:162
  35.8 130.0 %all-gather.4.cloned.1.call-done = bf16[1,2048,6144]{2,1,0:T(8,128)(2,1)} async-done(((bf16[1,128,6144]{2,1,0:T(8,128)(2,1)}), bf16[1,2048,6144]{2,1,0:T(8,128)(2,1)}) %all-gather.4.cloned.1.call-update) | async-done | bytes 25165840 | tf_op jit(solution)/shard_map/all_gather | solution.py:161
  165.8 29.7 %copy.95 = bf16[6144,2048]{1,0:T(8,128)(2,1)} copy(bf16[6144,2048]{0,1:T(8,128)(2,1)} %bitcast.357) | data formatting | bytes 50331648 | tf_op jit(solution)/shard_map/dot_general | solution.py:55
  217.8 316.0 %custom-call.6 = f32[4,16,1,64,64]{3,4,2,1,0:T(8,128)} custom-call(f32[4,16,1,64,64]{4,3,2,1,0:T(8,128)} %add_bitcast_fusion.1), custom_call_target="InvertDiagBlocksLowerTriangular" | custom-call | tf_op jit(solution)/shard_map/triangular_solve/custom-call.1 | solution.py:42
  543.2 41.3 %while.80 = (s32[]{:T(128)}, f32[16,128,128]{2,1,0:T(8,128)S(1)}, f32[16,128,128]{2,1,0:T(8,128)S(1)}, s32[4]{0:T(128)S(1)}, s32[]{:T(128)}, /*index=5*/f32[4,16...) while((s32[]{:T(128)}, f32[16,128,128]{2,1,0:T(8,128)S(1)}, ...), condition=%wide.region_3.5_spmd.clone, body=%wide.region_2.4_spmd.clone.sunk | while | flops 807534592 | bytes 19400364 | solution.py:133
  584.6 464.3 %while.76 = (s32[]{:T(128)}, f32[2,16,128,128]{3,2,1,0:T(8,128)}, pred[]{:T(512)}, f32[16,128,128]{2,1,0:T(8,128)S(1)}, f32[16,128,128]{2,1,0:T(8,128)S(1)}, /*index=5*/f32[2,16,128,128]{3,2,1,0:T(8,128)}, s32[]{:T(128)}) while((s32[]{:T(128)}, f32[2,16,128,128]{3,2,1,0:T(8,128)}, pred[]{:T(512)}, f32[16,128,128]{2,1,0:T(8,128)S(1)}, ...), condition=%wide.region_5.7_spmd, body=%wide.region_4.6_spmd.sunk | while | flops 807665664 | bytes 26214544 | solution.py:187
  591.6 27.0 %collective-permute-done = bf16[2,16,128,128]{3,2,1,0:T(8,128)(2,1)} collective-permute-done((bf16[2,16,128,128]{3,2,1,0:T(8,128)(2,1)}, bf16[2,16,128,128]{3,2,1,0:T(8,128)(2,1)}, u32[]{:S(2)}, u32[]{:S(2)}) %collective-permute-start) | collective-permute-done | bytes 1048608 | tf_op jit(solution)/shard_map/while/body/eval_jaxpr/ppermute | solution.py:16
  628.4 26.4 %collective-permute-done = bf16[2,16,128,128]{3,2,1,0:T(8,128)(2,1)} collective-permute-done((bf16[2,16,128,128]{3,2,1,0:T(8,128)(2,1)}, bf16[2,16,128,128]{3,2,1,0:T(8,128)(2,1)}, u32[]{:S(2)}, u32[]{:S(2)}) %collective-permute-start) | collective-permute-done | bytes 1048608 | tf_op jit(solution)/shard_map/while/body/eval_jaxpr/ppermute | solution.py:16
  664.5 25.5 %collective-permute-done = bf16[2,16,128,128]{3,2,1,0:T(8,128)(2,1)} collective-permute-done((bf16[2,16,128,128]{3,2,1,0:T(8,128)(2,1)}, bf16[2,16,128,128]{3,2,1,0:T(8,128)(2,1)}, u32[]{:S(2)}, u32[]{:S(2)}) %collective-permute-start) | collective-permute-done | bytes 1048608 | tf_op jit(solution)/shard_map/while/body/eval_jaxpr/ppermute | solution.py:16
  699.7 24.6 %collective-permute-done = bf16[2,16,128,128]{3,2,1,0:T(8,128)(2,1)} collective-permute-done((bf16[2,16,128,128]{3,2,1,0:T(8,128)(2,1)}, bf16[2,16,128,128]{3,2,1,0:T(8,128)(2,1)}, u32[]{:S(2)}, u32[]{:S(2)}) %collective-permute-start) | collective-permute-done | bytes 1048608 | tf_op jit(solution)/shard_map/while/body/eval_jaxpr/ppermute | solution.py:16
  734.0 23.6 %collective-permute-done = bf16[2,16,128,128]{3,2,1,0:T(8,128)(2,1)} collective-permute-done((bf16[2,16,128,128]{3,2,1,0:T(8,128)(2,1)}, bf16[2,16,128,128]{3,2,1,0:T(8,128)(2,1)}, u32[]{:S(2)}, u32[]{:S(2)}) %collective-permute-start) | collective-permute-done | bytes 1048608 | tf_op jit(solution)/shard_map/while/body/eval_jaxpr/ppermute | solution.py:16
  767.3 22.7 %collective-permute-done = bf16[2,16,128,128]{3,2,1,0:T(8,128)(2,1)} collective-permute-done((bf16[2,16,128,128]{3,2,1,0:T(8,128)(2,1)}, bf16[2,16,128,128]{3,2,1,0:T(8,128)(2,1)}, u32[]{:S(2)}, u32[]{:S(2)}) %collective-permute-start) | collective-permute-done | bytes 1048608 | tf_op jit(solution)/shard_map/while/body/eval_jaxpr/ppermute | solution.py:16
  799.8 21.8 %collective-permute-done = bf16[2,16,128,128]{3,2,1,0:T(8,128)(2,1)} collective-permute-done((bf16[2,16,128,128]{3,2,1,0:T(8,128)(2,1)}, bf16[2,16,128,128]{3,2,1,0:T(8,128)(2,1)}, u32[]{:S(2)}, u32[]{:S(2)}) %collective-permute-start) | collective-permute-done | bytes 1048608 | tf_op jit(solution)/shard_map/while/body/eval_jaxpr/ppermute | solution.py:16
  831.3 20.9 %collective-permute-done = bf16[2,16,128,128]{3,2,1,0:T(8,128)(2,1)} collective-permute-done((bf16[2,16,128,128]{3,2,1,0:T(8,128)(2,1)}, bf16[2,16,128,128]{3,2,1,0:T(8,128)(2,1)}, u32[]{:S(2)}, u32[]{:S(2)}) %collective-permute-start) | collective-permute-done | bytes 1048608 | tf_op jit(solution)/shard_map/while/body/eval_jaxpr/ppermute | solution.py:16
  861.8 20.0 collective-permute-done
  891.5 19.0 collective-permute-done
  920.2 18.1 collective-permute-done
  1055.1 48.0 %while.78 = (s32[]{:T(128)}, f32[16,128,128]{2,1,0:T(8,128)S(1)}, f32[4,16,64,128]{3,2,1,0:T(8,128)}, s32[4]{0:T(128)S(1)}, s32[]{:T(128)}, /*index=5*/f32[4,16,...) while((s32[]{:T(128)}, f32[16,128,128]{2,1,0:T(8,128)S(1)}, ...), condition=%wide.region_8.10_spmd.clone, body=%wide.region_7.9_spmd.clone.sunk | while | flops 806690816 | bytes 19451036 | solution.py:100
  1161.5 316.2 %custom-call.7 = f32[4,16,1,64,64]{3,4,2,1,0:T(8,128)} custom-call(f32[4,16,1,64,64]{4,3,2,1,0:T(8,128)} %add_bitcast_fusion), custom_call_target="InvertDiagBlocksLowerTriangular" | custom-call | tf_op jit(solution)/shard_map/triangular_solve/custom-call.1 | solution.py:42
  1487.0 54.6 %while.81 = (s32[]{:T(128)}, f32[16,128,128]{2,1,0:T(8,128)S(1)}, f32[16,128,128]{2,1,0:T(8,128)}, s32[4]{0:T(128)S(1)}, s32[]{:T(128)}, /*index=5*/f32[4,16,64,...) while((s32[]{:T(128)}, f32[16,128,128]{2,1,0:T(8,128)S(1)}, ...), condition=%wide.region_13.15_spmd.clone, body=%wide.region_12.14_spmd.clone.sunk | while | flops 807534592 | bytes 19401408 | solution.py:133
  1545.3 471.8 %while.77 = (s32[]{:T(128)}, f32[2,16,128,128]{3,2,1,0:T(8,128)}, pred[]{:T(512)}, f32[16,128,128]{2,1,0:T(8,128)S(1)}, f32[16,128,128]{2,1,0:T(8,128)}, /*index=5*/f32[2,16,128,128]{3,2,1,0:T(8,128)S(1)}, s32[]{:T(128)}) while((s32[]{:T(128)}, f32[2,16,128,128]{3,2,1,0:T(8,128)}, pred[]{:T(512)}, f32[16,128,128]{2,1,0:T(8,128)S(1)}, ...), condition=%wide.region_15.17_spmd, body=%wide.region_14.16_spmd.sunk | while | flops 807665664 | bytes 22020240 | solution.py:187
  1553.4 26.6 %collective-permute-done.1 = bf16[2,16,128,128]{3,2,1,0:T(8,128)(2,1)} collective-permute-done((bf16[2,16,128,128]{3,2,1,0:T(8,128)(2,1)}, bf16[2,16,128,128]{3,2,1,0:T(8,128)(2,1)}, u32[]{:S(2)}, u32[]{:S(2)}) %collective-permute-start.1) | collective-permute-done | bytes 1048608 | tf_op jit(solution)/shard_map/while/body/eval_jaxpr/ppermute | solution.py:16
  1590.7 25.7 %collective-permute-done.1 = bf16[2,16,128,128]{3,2,1,0:T(8,128)(2,1)} collective-permute-done((bf16[2,16,128,128]{3,2,1,0:T(8,128)(2,1)}, bf16[2,16,128,128]{3,2,1,0:T(8,128)(2,1)}, u32[]{:S(2)}, u32[]{:S(2)}) %collective-permute-start.1) | collective-permute-done | bytes 1048608 | tf_op jit(solution)/shard_map/while/body/eval_jaxpr/ppermute | solution.py:16
  1627.1 24.8 %collective-permute-done.1 = bf16[2,16,128,128]{3,2,1,0:T(8,128)(2,1)} collective-permute-done((bf16[2,16,128,128]{3,2,1,0:T(8,128)(2,1)}, bf16[2,16,128,128]{3,2,1,0:T(8,128)(2,1)}, u32[]{:S(2)}, u32[]{:S(2)}) %collective-permute-start.1) | collective-permute-done | bytes 1048608 | tf_op jit(solution)/shard_map/while/body/eval_jaxpr/ppermute | solution.py:16
  1662.6 23.8 %collective-permute-done.1 = bf16[2,16,128,128]{3,2,1,0:T(8,128)(2,1)} collective-permute-done((bf16[2,16,128,128]{3,2,1,0:T(8,128)(2,1)}, bf16[2,16,128,128]{3,2,1,0:T(8,128)(2,1)}, u32[]{:S(2)}, u32[]{:S(2)}) %collective-permute-start.1) | collective-permute-done | bytes 1048608 | tf_op jit(solution)/shard_map/while/body/eval_jaxpr/ppermute | solution.py:16
  1697.2 22.9 %collective-permute-done.1 = bf16[2,16,128,128]{3,2,1,0:T(8,128)(2,1)} collective-permute-done((bf16[2,16,128,128]{3,2,1,0:T(8,128)(2,1)}, bf16[2,16,128,128]{3,2,1,0:T(8,128)(2,1)}, u32[]{:S(2)}, u32[]{:S(2)}) %collective-permute-start.1) | collective-permute-done | bytes 1048608 | tf_op jit(solution)/shard_map/while/body/eval_jaxpr/ppermute | solution.py:16
  1730.8 22.0 %collective-permute-done.1 = bf16[2,16,128,128]{3,2,1,0:T(8,128)(2,1)} collective-permute-done((bf16[2,16,128,128]{3,2,1,0:T(8,128)(2,1)}, bf16[2,16,128,128]{3,2,1,0:T(8,128)(2,1)}, u32[]{:S(2)}, u32[]{:S(2)}) %collective-permute-start.1) | collective-permute-done | bytes 1048608 | tf_op jit(solution)/shard_map/while/body/eval_jaxpr/ppermute | solution.py:16
  1763.6 21.1 %collective-permute-done.1 = bf16[2,16,128,128]{3,2,1,0:T(8,128)(2,1)} collective-permute-done((bf16[2,16,128,128]{3,2,1,0:T(8,128)(2,1)}, bf16[2,16,128,128]{3,2,1,0:T(8,128)(2,1)}, u32[]{:S(2)}, u32[]{:S(2)}) %collective-permute-start.1) | collective-permute-done | bytes 1048608 | tf_op jit(solution)/shard_map/while/body/eval_jaxpr/ppermute | solution.py:16
  1795.3 20.1 collective-permute-done.1
  1826.2 19.2 collective-permute-done.1
  1856.2 18.3 collective-permute-done.1
  2021.2 44.4 %while.79 = (s32[]{:T(128)}, f32[16,128,128]{2,1,0:T(8,128)S(1)}, f32[4,16,64,128]{3,2,1,0:T(8,128)}, s32[4]{0:T(128)S(1)}, s32[]{:T(128)}, /*index=5*/f32[4,16,...) while((s32[]{:T(128)}, f32[16,128,128]{2,1,0:T(8,128)S(1)}, ...), condition=%wide.region_19.21_spmd.clone, body=%wide.region_18.20_spmd.clone.sunk | while | flops 806690816 | bytes 12109449 | solution.py:100
  (469 shorter events, 752.6 us)
Async XLA Ops:
  6.5 159.2 %all-gather.4.cloned.1.call-start = ((), (), s32[]{:S(2)}) async-start(), calls=%async_computation.1 | async-start | bytes 26738688 | tf_op jit(solution)/shard_map/all_gather | solution.py:161
  7.3 1538.0 %all-reduce.3.cloned.1.call-start = ((), (), s32[]{:S(2)}) async-start(), calls=%async_computation | async-start | bytes 1048576 | tf_op jit(solution)/shard_map/psum | solution.py:21
  589.4 29.2 %collective-permute-start = (bf16[2,16,128,128]{3,2,1,0:T(8,128)(2,1)}, bf16[2,16,128,128]{3,2,1,0:T(8,128)(2,1)}, u32[]{:S(2)}, u32[]{:S(2)}) collective-permute-start(bf16[2,16,128,128]{3,2,1,0:T(8,128)(2,1)} %pad_maximum_fusion.4), channel_id=1, source_target_pairs={{0,1},{1,2},{2,3},{3,4},{4,5},{5,6},{6,7},{7,8},{8,9},{9,10},{10,1... | collective-permute-start | bytes 3145736 | tf_op jit(solution)/shard_map/while/body/eval_jaxpr/ppermute | solution.py:16
  626.4 28.3 %collective-permute-start = (bf16[2,16,128,128]{3,2,1,0:T(8,128)(2,1)}, bf16[2,16,128,128]{3,2,1,0:T(8,128)(2,1)}, u32[]{:S(2)}, u32[]{:S(2)}) collective-permute-start(bf16[2,16,128,128]{3,2,1,0:T(8,128)(2,1)} %pad_maximum_fusion.4), channel_id=1, source_target_pairs={{0,1},{1,2},{2,3},{3,4},{4,5},{5,6},{6,7},{7,8},{8,9},{9,10},{10,1... | collective-permute-start | bytes 3145736 | tf_op jit(solution)/shard_map/while/body/eval_jaxpr/ppermute | solution.py:16
  662.6 27.4 %collective-permute-start = (bf16[2,16,128,128]{3,2,1,0:T(8,128)(2,1)}, bf16[2,16,128,128]{3,2,1,0:T(8,128)(2,1)}, u32[]{:S(2)}, u32[]{:S(2)}) collective-permute-start(bf16[2,16,128,128]{3,2,1,0:T(8,128)(2,1)} %pad_maximum_fusion.4), channel_id=1, source_target_pairs={{0,1},{1,2},{2,3},{3,4},{4,5},{5,6},{6,7},{7,8},{8,9},{9,10},{10,1... | collective-permute-start | bytes 3145736 | tf_op jit(solution)/shard_map/while/body/eval_jaxpr/ppermute | solution.py:16
  697.8 26.5 %collective-permute-start = (bf16[2,16,128,128]{3,2,1,0:T(8,128)(2,1)}, bf16[2,16,128,128]{3,2,1,0:T(8,128)(2,1)}, u32[]{:S(2)}, u32[]{:S(2)}) collective-permute-start(bf16[2,16,128,128]{3,2,1,0:T(8,128)(2,1)} %pad_maximum_fusion.4), channel_id=1, source_target_pairs={{0,1},{1,2},{2,3},{3,4},{4,5},{5,6},{6,7},{7,8},{8,9},{9,10},{10,1... | collective-permute-start | bytes 3145736 | tf_op jit(solution)/shard_map/while/body/eval_jaxpr/ppermute | solution.py:16
  732.0 25.6 %collective-permute-start = (bf16[2,16,128,128]{3,2,1,0:T(8,128)(2,1)}, bf16[2,16,128,128]{3,2,1,0:T(8,128)(2,1)}, u32[]{:S(2)}, u32[]{:S(2)}) collective-permute-start(bf16[2,16,128,128]{3,2,1,0:T(8,128)(2,1)} %pad_maximum_fusion.4), channel_id=1, source_target_pairs={{0,1},{1,2},{2,3},{3,4},{4,5},{5,6},{6,7},{7,8},{8,9},{9,10},{10,1... | collective-permute-start | bytes 3145736 | tf_op jit(solution)/shard_map/while/body/eval_jaxpr/ppermute | solution.py:16
  765.4 24.6 %collective-permute-start = (bf16[2,16,128,128]{3,2,1,0:T(8,128)(2,1)}, bf16[2,16,128,128]{3,2,1,0:T(8,128)(2,1)}, u32[]{:S(2)}, u32[]{:S(2)}) collective-permute-start(bf16[2,16,128,128]{3,2,1,0:T(8,128)(2,1)} %pad_maximum_fusion.4), channel_id=1, source_target_pairs={{0,1},{1,2},{2,3},{3,4},{4,5},{5,6},{6,7},{7,8},{8,9},{9,10},{10,1... | collective-permute-start | bytes 3145736 | tf_op jit(solution)/shard_map/while/body/eval_jaxpr/ppermute | solution.py:16
  797.8 23.7 %collective-permute-start = (bf16[2,16,128,128]{3,2,1,0:T(8,128)(2,1)}, bf16[2,16,128,128]{3,2,1,0:T(8,128)(2,1)}, u32[]{:S(2)}, u32[]{:S(2)}) collective-permute-start(bf16[2,16,128,128]{3,2,1,0:T(8,128)(2,1)} %pad_maximum_fusion.4), channel_id=1, source_target_pairs={{0,1},{1,2},{2,3},{3,4},{4,5},{5,6},{6,7},{7,8},{8,9},{9,10},{10,1... | collective-permute-start | bytes 3145736 | tf_op jit(solution)/shard_map/while/body/eval_jaxpr/ppermute | solution.py:16
  829.3 22.8 %collective-permute-start = (bf16[2,16,128,128]{3,2,1,0:T(8,128)(2,1)}, bf16[2,16,128,128]{3,2,1,0:T(8,128)(2,1)}, u32[]{:S(2)}, u32[]{:S(2)}) collective-permute-start(bf16[2,16,128,128]{3,2,1,0:T(8,128)(2,1)} %pad_maximum_fusion.4), channel_id=1, source_target_pairs={{0,1},{1,2},{2,3},{3,4},{4,5},{5,6},{6,7},{7,8},{8,9},{9,10},{10,1... | collective-permute-start | bytes 3145736 | tf_op jit(solution)/shard_map/while/body/eval_jaxpr/ppermute | solution.py:16
  859.9 21.9 %collective-permute-start = (bf16[2,16,128,128]{3,2,1,0:T(8,128)(2,1)}, bf16[2,16,128,128]{3,2,1,0:T(8,128)(2,1)}, u32[]{:S(2)}, u32[]{:S(2)}) collective-permute-start(bf16[2,16,128,128]{3,2,1,0:T(8,128)(2,1)} %pad_maximum_fusion.4), channel_id=1, source_target_pairs={{0,1},{1,2},{2,3},{3,4},{4,5},{5,6},{6,7},{7,8},{8,9},{9,10},{10,1... | collective-permute-start | bytes 3145736 | tf_op jit(solution)/shard_map/while/body/eval_jaxpr/ppermute | solution.py:16
  889.6 20.9 %collective-permute-start = (bf16[2,16,128,128]{3,2,1,0:T(8,128)(2,1)}, bf16[2,16,128,128]{3,2,1,0:T(8,128)(2,1)}, u32[]{:S(2)}, u32[]{:S(2)}) collective-permute-start(bf16[2,16,128,128]{3,2,1,0:T(8,128)(2,1)} %pad_maximum_fusion.4), channel_id=1, source_target_pairs={{0,1},{1,2},{2,3},{3,4},{4,5},{5,6},{6,7},{7,8},{8,9},{9,10},{10,1... | collective-permute-start | bytes 3145736 | tf_op jit(solution)/shard_map/while/body/eval_jaxpr/ppermute | solution.py:16
  918.3 20.0 collective-permute-start
  946.1 19.1 collective-permute-start
  973.0 19.1 collective-permute-start
  999.9 19.1 collective-permute-start
  1026.8 19.1 collective-permute-start
  1551.5 28.5 %collective-permute-start.1 = (bf16[2,16,128,128]{3,2,1,0:T(8,128)(2,1)}, bf16[2,16,128,128]{3,2,1,0:T(8,128)(2,1)}, u32[]{:S(2)}, u32[]{:S(2)}) collective-permute-start(bf16[2,16,128,128]{3,2,1,0:T(8,128)(2,1)} %pad_maximum_fusion.5), channel_id=1, source_target_pairs={{0,1},{1,2},{2,3},{3,4},{4,5},{5,6},{6,7},{7,8},{8,9},{9,10},{10,1... | collective-permute-start | bytes 3145736 | tf_op jit(solution)/shard_map/while/body/eval_jaxpr/ppermute | solution.py:16
  1588.8 27.6 %collective-permute-start.1 = (bf16[2,16,128,128]{3,2,1,0:T(8,128)(2,1)}, bf16[2,16,128,128]{3,2,1,0:T(8,128)(2,1)}, u32[]{:S(2)}, u32[]{:S(2)}) collective-permute-start(bf16[2,16,128,128]{3,2,1,0:T(8,128)(2,1)} %pad_maximum_fusion.5), channel_id=1, source_target_pairs={{0,1},{1,2},{2,3},{3,4},{4,5},{5,6},{6,7},{7,8},{8,9},{9,10},{10,1... | collective-permute-start | bytes 3145736 | tf_op jit(solution)/shard_map/while/body/eval_jaxpr/ppermute | solution.py:16
  1625.2 26.7 %collective-permute-start.1 = (bf16[2,16,128,128]{3,2,1,0:T(8,128)(2,1)}, bf16[2,16,128,128]{3,2,1,0:T(8,128)(2,1)}, u32[]{:S(2)}, u32[]{:S(2)}) collective-permute-start(bf16[2,16,128,128]{3,2,1,0:T(8,128)(2,1)} %pad_maximum_fusion.5), channel_id=1, source_target_pairs={{0,1},{1,2},{2,3},{3,4},{4,5},{5,6},{6,7},{7,8},{8,9},{9,10},{10,1... | collective-permute-start | bytes 3145736 | tf_op jit(solution)/shard_map/while/body/eval_jaxpr/ppermute | solution.py:16
  1660.7 25.8 %collective-permute-start.1 = (bf16[2,16,128,128]{3,2,1,0:T(8,128)(2,1)}, bf16[2,16,128,128]{3,2,1,0:T(8,128)(2,1)}, u32[]{:S(2)}, u32[]{:S(2)}) collective-permute-start(bf16[2,16,128,128]{3,2,1,0:T(8,128)(2,1)} %pad_maximum_fusion.5), channel_id=1, source_target_pairs={{0,1},{1,2},{2,3},{3,4},{4,5},{5,6},{6,7},{7,8},{8,9},{9,10},{10,1... | collective-permute-start | bytes 3145736 | tf_op jit(solution)/shard_map/while/body/eval_jaxpr/ppermute | solution.py:16
  1695.3 24.8 %collective-permute-start.1 = (bf16[2,16,128,128]{3,2,1,0:T(8,128)(2,1)}, bf16[2,16,128,128]{3,2,1,0:T(8,128)(2,1)}, u32[]{:S(2)}, u32[]{:S(2)}) collective-permute-start(bf16[2,16,128,128]{3,2,1,0:T(8,128)(2,1)} %pad_maximum_fusion.5), channel_id=1, source_target_pairs={{0,1},{1,2},{2,3},{3,4},{4,5},{5,6},{6,7},{7,8},{8,9},{9,10},{10,1... | collective-permute-start | bytes 3145736 | tf_op jit(solution)/shard_map/while/body/eval_jaxpr/ppermute | solution.py:16
  1728.9 23.9 %collective-permute-start.1 = (bf16[2,16,128,128]{3,2,1,0:T(8,128)(2,1)}, bf16[2,16,128,128]{3,2,1,0:T(8,128)(2,1)}, u32[]{:S(2)}, u32[]{:S(2)}) collective-permute-start(bf16[2,16,128,128]{3,2,1,0:T(8,128)(2,1)} %pad_maximum_fusion.5), channel_id=1, source_target_pairs={{0,1},{1,2},{2,3},{3,4},{4,5},{5,6},{6,7},{7,8},{8,9},{9,10},{10,1... | collective-permute-start | bytes 3145736 | tf_op jit(solution)/shard_map/while/body/eval_jaxpr/ppermute | solution.py:16
  1761.6 23.0 %collective-permute-start.1 = (bf16[2,16,128,128]{3,2,1,0:T(8,128)(2,1)}, bf16[2,16,128,128]{3,2,1,0:T(8,128)(2,1)}, u32[]{:S(2)}, u32[]{:S(2)}) collective-permute-start(bf16[2,16,128,128]{3,2,1,0:T(8,128)(2,1)} %pad_maximum_fusion.5), channel_id=1, source_target_pairs={{0,1},{1,2},{2,3},{3,4},{4,5},{5,6},{6,7},{7,8},{8,9},{9,10},{10,1... | collective-permute-start | bytes 3145736 | tf_op jit(solution)/shard_map/while/body/eval_jaxpr/ppermute | solution.py:16
  1793.4 22.1 %collective-permute-start.1 = (bf16[2,16,128,128]{3,2,1,0:T(8,128)(2,1)}, bf16[2,16,128,128]{3,2,1,0:T(8,128)(2,1)}, u32[]{:S(2)}, u32[]{:S(2)}) collective-permute-start(bf16[2,16,128,128]{3,2,1,0:T(8,128)(2,1)} %pad_maximum_fusion.5), channel_id=1, source_target_pairs={{0,1},{1,2},{2,3},{3,4},{4,5},{5,6},{6,7},{7,8},{8,9},{9,10},{10,1... | collective-permute-start | bytes 3145736 | tf_op jit(solution)/shard_map/while/body/eval_jaxpr/ppermute | solution.py:16
  1824.3 21.1 %collective-permute-start.1 = (bf16[2,16,128,128]{3,2,1,0:T(8,128)(2,1)}, bf16[2,16,128,128]{3,2,1,0:T(8,128)(2,1)}, u32[]{:S(2)}, u32[]{:S(2)}) collective-permute-start(bf16[2,16,128,128]{3,2,1,0:T(8,128)(2,1)} %pad_maximum_fusion.5), channel_id=1, source_target_pairs={{0,1},{1,2},{2,3},{3,4},{4,5},{5,6},{6,7},{7,8},{8,9},{9,10},{10,1... | collective-permute-start | bytes 3145736 | tf_op jit(solution)/shard_map/while/body/eval_jaxpr/ppermute | solution.py:16
  1854.3 20.2 collective-permute-start.1
  1883.3 19.3 collective-permute-start.1
  1911.4 19.1 collective-permute-start.1
  1939.3 19.1 collective-permute-start.1
  1967.2 19.1 collective-permute-start.1
  1995.2 19.1 collective-permute-start.1
  (64 other events, 1277.4 us)
Sparse Core Ops, SparseCore 0:
  9.5 156.2 all-gather.3
  1115.4 85.1 all-reduce.2
where the time goes:
time: 2100 us; the launch traced here: 2080 us
  other arithmetic  789 us (38%)
  waiting for transfers between devices  771 us (37%)
  matrix products  326 us (16%)
  local copies, waits for them, and re-layouts  74.7 us (4%)
  starting transfers between devices  57.7 us (3%)
  blocking collectives  24.4 us (1%)
  loops' own time  23.7 us (1%)
    another operation x5, other arithmetic, block_solve(): lax.linalg.triangular_solve(system, right_side, left_side=True, lower=Tru...  632 us
    ppermute x30, waiting for transfers between devices, from_behind(): return lax.ppermute(value, axis, pairs)  629 us
    all_gather x1, waiting for transfers between devices, shards(): lax.all_gather(w_qkv[0], 'seq', axis=0, tiled=True)  130 us
    select_n x30, other arithmetic, hop_once(): return jnp.where(position == 0, empty_map, passed)  87.6 us
    dot_general x30, matrix products, compose(): jnp.einsum('hij,hjk->hik', latter[0], earlier[0], precision=FULL_PRECISION)  74.3 us
    ppermute x30, starting transfers between devices, from_behind(): return lax.ppermute(value, axis, pairs)  57.6 us
    dot_general x30, matrix products, compose(): jnp.einsum('hij,hjk->hik', latter[0], earlier[1], precision=FULL_PRECISION)  54.3 us
  transfers between devices with their start and end apart: 33, of which 32 were waited for; matrix products, arithmetic and copies ran while one was open for 20% of the time, Pallas kernels for 0%

commit v1 on v0

--- a/solution.py
+++ b/solution.py
@@ -8,6 +8,14 @@
 GROUP = 64
 TICKS = 2
 FULL_PRECISION = lax.Precision.HIGHEST
+
+
+def tiled_gather(array, axis, dim):
+    length = lax.axis_size(axis)
+    repeats = [length if d == dim else 1 for d in range(array.ndim)]
+    return lax.all_to_all(
+        jnp.tile(array, repeats), axis, split_axis=dim, concat_axis=dim, tiled=True
+    )
 
 
 def from_behind(value, axis, by):
@@ -158,7 +166,7 @@
 
 def shards(residual, w_qkv, w_beta, beta_bias, norm_gain, out_gain, state_in, doc_start):
     weight_qkv, weight_beta = (
-        lax.all_gather(w_qkv[0], "seq", axis=0, tiled=True),
+        tiled_gather(w_qkv[0], "seq", 0),
         lax.all_gather(w_beta[0], "seq", axis=0, tiled=True),
     )
     seq_count = lax.axis_size("seq")

time: 2100 us -> 2340 us (1.11)
  blocking collectives: 24.4 us -> 389 us
  waiting for transfers between devices: 771 us -> 610 us
  local copies, waits for them, and re-layouts: 74.7 us -> 109 us
    all_gather x1, blocking collectives: 24.4 us -> 389 us  [shards(): lax.all_gather(w_beta[0], 'seq', axis=0, tiled=True)]
    all_gather x1 -> x0, waiting for transfers between devices: 130 us -> none  [shards(): lax.all_gather(w_qkv[0], 'seq', axis=0, tiled=True)]
    all_to_all x0 -> x1, local copies, waits for them, and re-layouts: none -> 31.3 us  [tiled_gather(): lax.all_to_all(jnp.tile(array, repeats), axis, split_axis=dim, concat_axi...]
    ppermute x30, waiting for transfers between devices: 629 us -> 598 us  [from_behind(): return lax.ppermute(value, axis, pairs)]
  transfers between devices with their start and end apart: 33 -> 33, of which waited for: 32 -> 31; matrix products, arithmetic and copies ran while one was open for 20% -> 17% of each run, Pallas kernels for 0% -> 0%
where the time goes in v1:
time: 2340 us; the launch traced here: 2320 us
  other arithmetic  787 us (34%)
  waiting for transfers between devices  610 us (26%)
  blocking collectives  389 us (17%)
  matrix products  325 us (14%)
  local copies, waits for them, and re-layouts  109 us (5%)
  starting transfers between devices  65.5 us (3%)
  loops' own time  24 us (1%)
    another operation x5, other arithmetic, block_solve(): lax.linalg.triangular_solve(system, right_side, left_side=True, lower=Tru...  632 us
    ppermute x30, waiting for transfers between devices, from_behind(): return lax.ppermute(value, axis, pairs)  598 us
    all_gather x1, blocking collectives, shards(): lax.all_gather(w_beta[0], 'seq', axis=0, tiled=True)  389 us
    select_n x30, other arithmetic, hop_once(): return jnp.where(position == 0, empty_map, passed)  87.8 us
    dot_general x30, matrix products, compose(): jnp.einsum('hij,hjk->hik', latter[0], earlier[0], precision=FULL_PRECISION)  74.3 us
    ppermute x30, starting transfers between devices, from_behind(): return lax.ppermute(value, axis, pairs)  57.3 us
    dot_general x30, matrix products, compose(): jnp.einsum('hij,hjk->hik', latter[0], earlier[1], precision=FULL_PRECISION)  54.3 us
  transfers between devices with their start and end apart: 33, of which 31 were waited for; matrix products, arithmetic and copies ran while one was open for 17% of the time, Pallas kernels for 0%

profile of v1, /device:TPU:34, one launch (start us, length us, event | category | flops | bytes accessed | tf_op | source)
XLA Modules:
  0.0 2323.5 jit_solution(5422136559978266999)
XLA Ops:
  25.6 388.5 %all-gather = bf16[1,2048,16]{1,2,0:T(8,128)(2,1)S(1)} all-gather(bf16[1,128,16]{1,2,0:T(8,128)(2,1)S(1)} %copy-done.18), channel_id=2, replica_groups=mesh['section'=8,'seq'=16] {'seq'}, dimensions={1}, use_global_device_ids=true | all-gather | bytes 69632 | tf_op jit(solution)/shard_map/all_gather | solution.py:170
  418.1 31.3 %copy.60 = bf16[16,128,6144]{2,1,0:T(8,128)(2,1)} copy(bf16[16,128,6144]{1,2,0:T(8,128)(2,1)} %all-to-all-done) | data formatting | bytes 50331648 | tf_op jit(solution)/shard_map/all_to_all | solution.py:16
  449.4 31.7 %copy.61 = bf16[6144,2048]{1,0:T(8,128)(2,1)} copy(bf16[6144,2048]{0,1:T(8,128)(2,1)} %bitcast.352) | data formatting | bytes 50331648 | tf_op jit(solution)/shard_map/dot_general | solution.py:63
  503.4 316.0 %custom-call.6 = f32[4,16,1,64,64]{3,4,2,1,0:T(8,128)} custom-call(f32[4,16,1,64,64]{4,3,2,1,0:T(8,128)} %add_bitcast_fusion.1), custom_call_target="InvertDiagBlocksLowerTriangular" | custom-call | tf_op jit(solution)/shard_map/triangular_solve/custom-call.1 | solution.py:50
  828.8 41.9 %while.80 = (s32[]{:T(128)}, f32[16,128,128]{2,1,0:T(8,128)S(1)}, f32[16,128,128]{2,1,0:T(8,128)S(1)}, s32[4]{0:T(128)S(1)}, s32[]{:T(128)}, /*index=5*/f32[4,16...) while((s32[]{:T(128)}, f32[16,128,128]{2,1,0:T(8,128)S(1)}, ...), condition=%wide.region_3.5_spmd.clone, body=%wide.region_2.4_spmd.clone.sunk | while | flops 807534592 | bytes 19400364 | solution.py:141
  870.8 433.5 %while.76 = (s32[]{:T(128)}, f32[2,16,128,128]{3,2,1,0:T(8,128)}, pred[]{:T(512)}, f32[16,128,128]{2,1,0:T(8,128)S(1)}, f32[16,128,128]{2,1,0:T(8,128)S(1)}, /*index=5*/f32[2,16,128,128]{3,2,1,0:T(8,128)}, s32[]{:T(128)}) while((s32[]{:T(128)}, f32[2,16,128,128]{3,2,1,0:T(8,128)}, pred[]{:T(512)}, f32[16,128,128]{2,1,0:T(8,128)S(1)}, ...), condition=%wide.region_5.7_spmd, body=%wide.region_4.6_spmd.sunk | while | flops 807665664 | bytes 26214544 | solution.py:195
  877.5 22.0 collective-permute-done
  909.2 21.0 collective-permute-done
  939.9 20.1 collective-permute-done
  969.8 19.2 collective-permute-done
  998.6 18.3 collective-permute-done
  1134.4 18.1 collective-permute-done
  1162.2 19.1 collective-permute-done
  1191.0 20.2 collective-permute-done
  1221.0 21.3 collective-permute-done
  1252.0 22.4 collective-permute-done
  1310.4 48.2 %while.78 = (s32[]{:T(128)}, f32[16,128,128]{2,1,0:T(8,128)S(1)}, f32[4,16,64,128]{3,2,1,0:T(8,128)}, s32[4]{0:T(128)S(1)}, s32[]{:T(128)}, /*index=5*/f32[4,16,...) while((s32[]{:T(128)}, f32[16,128,128]{2,1,0:T(8,128)S(1)}, ...), condition=%wide.region_8.10_spmd.clone, body=%wide.region_7.9_spmd.clone.sunk | while | flops 806690816 | bytes 19451036 | solution.py:108
  1409.7 316.0 %custom-call.7 = f32[4,16,1,64,64]{3,4,2,1,0:T(8,128)} custom-call(f32[4,16,1,64,64]{4,3,2,1,0:T(8,128)} %add_bitcast_fusion), custom_call_target="InvertDiagBlocksLowerTriangular" | custom-call | tf_op jit(solution)/shard_map/triangular_solve/custom-call.1 | solution.py:50
  1735.0 54.6 %while.81 = (s32[]{:T(128)}, f32[16,128,128]{2,1,0:T(8,128)S(1)}, f32[16,128,128]{2,1,0:T(8,128)}, s32[4]{0:T(128)S(1)}, s32[]{:T(128)}, /*index=5*/f32[4,16,64,...) while((s32[]{:T(128)}, f32[16,128,128]{2,1,0:T(8,128)S(1)}, ...), condition=%wide.region_13.15_spmd.clone, body=%wide.region_12.14_spmd.clone.sunk | while | flops 807534592 | bytes 19401408 | solution.py:141
  1792.7 471.6 %while.77 = (s32[]{:T(128)}, f32[2,16,128,128]{3,2,1,0:T(8,128)}, pred[]{:T(512)}, f32[16,128,128]{2,1,0:T(8,128)S(1)}, f32[16,128,128]{2,1,0:T(8,128)}, /*index=5*/f32[2,16,128,128]{3,2,1,0:T(8,128)S(1)}, s32[]{:T(128)}) while((s32[]{:T(128)}, f32[2,16,128,128]{3,2,1,0:T(8,128)}, pred[]{:T(512)}, f32[16,128,128]{2,1,0:T(8,128)S(1)}, ...), condition=%wide.region_15.17_spmd, body=%wide.region_14.16_spmd.sunk | while | flops 807665664 | bytes 22020240 | solution.py:195
  1800.6 26.6 %collective-permute-done.1 = bf16[2,16,128,128]{3,2,1,0:T(8,128)(2,1)} collective-permute-done((bf16[2,16,128,128]{3,2,1,0:T(8,128)(2,1)}, bf16[2,16,128,128]{3,2,1,0:T(8,128)(2,1)}, u32[]{:S(2)}, u32[]{:S(2)}) %collective-permute-start.1) | collective-permute-done | bytes 1048608 | tf_op jit(solution)/shard_map/while/body/eval_jaxpr/ppermute | solution.py:24
  1837.9 25.7 %collective-permute-done.1 = bf16[2,16,128,128]{3,2,1,0:T(8,128)(2,1)} collective-permute-done((bf16[2,16,128,128]{3,2,1,0:T(8,128)(2,1)}, bf16[2,16,128,128]{3,2,1,0:T(8,128)(2,1)}, u32[]{:S(2)}, u32[]{:S(2)}) %collective-permute-start.1) | collective-permute-done | bytes 1048608 | tf_op jit(solution)/shard_map/while/body/eval_jaxpr/ppermute | solution.py:24
  1874.3 24.8 %collective-permute-done.1 = bf16[2,16,128,128]{3,2,1,0:T(8,128)(2,1)} collective-permute-done((bf16[2,16,128,128]{3,2,1,0:T(8,128)(2,1)}, bf16[2,16,128,128]{3,2,1,0:T(8,128)(2,1)}, u32[]{:S(2)}, u32[]{:S(2)}) %collective-permute-start.1) | collective-permute-done | bytes 1048608 | tf_op jit(solution)/shard_map/while/body/eval_jaxpr/ppermute | solution.py:24
  1909.8 23.8 %collective-permute-done.1 = bf16[2,16,128,128]{3,2,1,0:T(8,128)(2,1)} collective-permute-done((bf16[2,16,128,128]{3,2,1,0:T(8,128)(2,1)}, bf16[2,16,128,128]{3,2,1,0:T(8,128)(2,1)}, u32[]{:S(2)}, u32[]{:S(2)}) %collective-permute-start.1) | collective-permute-done | bytes 1048608 | tf_op jit(solution)/shard_map/while/body/eval_jaxpr/ppermute | solution.py:24
  1944.3 22.9 collective-permute-done.1
  1978.0 22.0 collective-permute-done.1
  2010.7 21.1 collective-permute-done.1
  2042.5 20.1 collective-permute-done.1
  2073.4 19.2 collective-permute-done.1
  2103.3 18.3 collective-permute-done.1
  2132.4 17.4 collective-permute-done.1
  2268.4 39.6 %while.79 = (s32[]{:T(128)}, f32[16,128,128]{2,1,0:T(8,128)S(1)}, f32[4,16,64,128]{3,2,1,0:T(8,128)}, s32[4]{0:T(128)S(1)}, s32[]{:T(128)}, /*index=5*/f32[4,16,...) while((s32[]{:T(128)}, f32[16,128,128]{2,1,0:T(8,128)S(1)}, ...), condition=%wide.region_19.21_spmd.clone, body=%wide.region_18.20_spmd.clone.sunk | while | flops 806690816 | bytes 19451036 | solution.py:108
  (467 shorter events, 758.1 us)
Async XLA Ops:
  17.3 400.8 %all-to-all-start = ((bf16[16,128,6144]{1,2,0:T(8,128)(2,1)}), bf16[16,128,6144]{1,2,0:T(8,128)(2,1)}, u32[]{:S(2)}, u32[]{:S(2)}) async-start(bf16[16,128,6144]{1,2,0:T(8,128)(2,1)} %tile.9), calls=%async_computation | async-start | bytes 50331648 | tf_op jit(solution)/shard_map/all_to_all | solution.py:16
  25.5 1767.2 %all-reduce.3.cloned.1.call-start = ((), (), s32[]{:S(2)}) async-start(), calls=%async_computation.1 | async-start | bytes 1048576 | tf_op jit(solution)/shard_map/psum | solution.py:29
  875.6 23.9 %collective-permute-start = (bf16[2,16,128,128]{3,2,1,0:T(8,128)(2,1)}, bf16[2,16,128,128]{3,2,1,0:T(8,128)(2,1)}, u32[]{:S(2)}, u32[]{:S(2)}) collective-permute-start(bf16[2,16,128,128]{3,2,1,0:T(8,128)(2,1)} %pad_maximum_fusion.4), channel_id=1, source_target_pairs={{0,1},{1,2},{2,3},{3,4},{4,5},{5,6},{6,7},{7,8},{8,9},{9,10},{10,1... | collective-permute-start | bytes 3145736 | tf_op jit(solution)/shard_map/while/body/eval_jaxpr/ppermute | solution.py:24
  907.3 22.9 collective-permute-start
  938.0 22.0 collective-permute-start
  967.8 21.1 collective-permute-start
  996.7 20.2 collective-permute-start
  1024.7 19.3 collective-permute-start
  1051.8 19.1 collective-permute-start
  1078.7 19.1 collective-permute-start
  1105.6 19.1 collective-permute-start
  1132.5 20.0 collective-permute-start
  1160.2 21.1 collective-permute-start
  1189.1 22.1 collective-permute-start
  1219.0 23.2 collective-permute-start
  1250.0 24.3 %collective-permute-start = (bf16[2,16,128,128]{3,2,1,0:T(8,128)(2,1)}, bf16[2,16,128,128]{3,2,1,0:T(8,128)(2,1)}, u32[]{:S(2)}, u32[]{:S(2)}) collective-permute-start(bf16[2,16,128,128]{3,2,1,0:T(8,128)(2,1)} %pad_maximum_fusion.4), channel_id=1, source_target_pairs={{0,1},{1,2},{2,3},{3,4},{4,5},{5,6},{6,7},{7,8},{8,9},{9,10},{10,1... | collective-permute-start | bytes 3145736 | tf_op jit(solution)/shard_map/while/body/eval_jaxpr/ppermute | solution.py:24
  1282.1 19.1 collective-permute-start
  1798.6 28.5 %collective-permute-start.1 = (bf16[2,16,128,128]{3,2,1,0:T(8,128)(2,1)}, bf16[2,16,128,128]{3,2,1,0:T(8,128)(2,1)}, u32[]{:S(2)}, u32[]{:S(2)}) collective-permute-start(bf16[2,16,128,128]{3,2,1,0:T(8,128)(2,1)} %pad_maximum_fusion.5), channel_id=1, source_target_pairs={{0,1},{1,2},{2,3},{3,4},{4,5},{5,6},{6,7},{7,8},{8,9},{9,10},{10,1... | collective-permute-start | bytes 3145736 | tf_op jit(solution)/shard_map/while/body/eval_jaxpr/ppermute | solution.py:24
  1836.0 27.6 %collective-permute-start.1 = (bf16[2,16,128,128]{3,2,1,0:T(8,128)(2,1)}, bf16[2,16,128,128]{3,2,1,0:T(8,128)(2,1)}, u32[]{:S(2)}, u32[]{:S(2)}) collective-permute-start(bf16[2,16,128,128]{3,2,1,0:T(8,128)(2,1)} %pad_maximum_fusion.5), channel_id=1, source_target_pairs={{0,1},{1,2},{2,3},{3,4},{4,5},{5,6},{6,7},{7,8},{8,9},{9,10},{10,1... | collective-permute-start | bytes 3145736 | tf_op jit(solution)/shard_map/while/body/eval_jaxpr/ppermute | solution.py:24
  1872.4 26.7 %collective-permute-start.1 = (bf16[2,16,128,128]{3,2,1,0:T(8,128)(2,1)}, bf16[2,16,128,128]{3,2,1,0:T(8,128)(2,1)}, u32[]{:S(2)}, u32[]{:S(2)}) collective-permute-start(bf16[2,16,128,128]{3,2,1,0:T(8,128)(2,1)} %pad_maximum_fusion.5), channel_id=1, source_target_pairs={{0,1},{1,2},{2,3},{3,4},{4,5},{5,6},{6,7},{7,8},{8,9},{9,10},{10,1... | collective-permute-start | bytes 3145736 | tf_op jit(solution)/shard_map/while/body/eval_jaxpr/ppermute | solution.py:24
  1907.9 25.8 %collective-permute-start.1 = (bf16[2,16,128,128]{3,2,1,0:T(8,128)(2,1)}, bf16[2,16,128,128]{3,2,1,0:T(8,128)(2,1)}, u32[]{:S(2)}, u32[]{:S(2)}) collective-permute-start(bf16[2,16,128,128]{3,2,1,0:T(8,128)(2,1)} %pad_maximum_fusion.5), channel_id=1, source_target_pairs={{0,1},{1,2},{2,3},{3,4},{4,5},{5,6},{6,7},{7,8},{8,9},{9,10},{10,1... | collective-permute-start | bytes 3145736 | tf_op jit(solution)/shard_map/while/body/eval_jaxpr/ppermute | solution.py:24
  1942.4 24.8 %collective-permute-start.1 = (bf16[2,16,128,128]{3,2,1,0:T(8,128)(2,1)}, bf16[2,16,128,128]{3,2,1,0:T(8,128)(2,1)}, u32[]{:S(2)}, u32[]{:S(2)}) collective-permute-start(bf16[2,16,128,128]{3,2,1,0:T(8,128)(2,1)} %pad_maximum_fusion.5), channel_id=1, source_target_pairs={{0,1},{1,2},{2,3},{3,4},{4,5},{5,6},{6,7},{7,8},{8,9},{9,10},{10,1... | collective-permute-start | bytes 3145736 | tf_op jit(solution)/shard_map/while/body/eval_jaxpr/ppermute | solution.py:24
  1976.1 23.9 %collective-permute-start.1 = (bf16[2,16,128,128]{3,2,1,0:T(8,128)(2,1)}, bf16[2,16,128,128]{3,2,1,0:T(8,128)(2,1)}, u32[]{:S(2)}, u32[]{:S(2)}) collective-permute-start(bf16[2,16,128,128]{3,2,1,0:T(8,128)(2,1)} %pad_maximum_fusion.5), channel_id=1, source_target_pairs={{0,1},{1,2},{2,3},{3,4},{4,5},{5,6},{6,7},{7,8},{8,9},{9,10},{10,1... | collective-permute-start | bytes 3145736 | tf_op jit(solution)/shard_map/while/body/eval_jaxpr/ppermute | solution.py:24
  2008.8 23.0 collective-permute-start.1
  2040.6 22.1 collective-permute-start.1
  2071.5 21.1 collective-permute-start.1
  2101.4 20.2 collective-permute-start.1
  2130.5 19.3 collective-permute-start.1
  2158.6 19.1 collective-permute-start.1
  2186.5 19.1 collective-permute-start.1
  2214.4 19.1 collective-permute-start.1
  2242.3 19.1 collective-permute-start.1
  (67 other events, 2661.4 us)
Sparse Core Ops, SparseCore 0:
  1371.0 84.1 all-reduce.2
